TPU v7x, 256 devices: a whole 4x4x8 slice. The times are simulated.
256 devices in a mesh: segment: 4 (over y_lo, core), dp: 64 (over z, x, y_hi).
Axes of the slice: x: 4, y: 4 (y_hi: 2, y_lo: 2; y = y_hi * 2 + y_lo), z: 8, core: 2. Of those that a mesh axis runs over, the one named last changes fastest.
Arguments:
- images: bfloat16 [512, 256, 1024], P('dp'), may hold values from -6 to 6
- texts: bfloat16 [512, 64, 1536], P('dp'), may hold values from -6 to 6
- section_weights: bfloat16 [4, 21504, 128], P('segment'), may hold values from -0.15625 to 0.15625
- uniting_weights: bfloat16 [3584, 1024], P('dp'), may hold values from -0.125 to 0.125
- codebooks: float32 [64, 2, 256, 1024], P('dp'), may hold values from -3 to 3
- neg_bank: bfloat16 [64, 256, 1024], P('dp'), may hold values from -6 to 6
- item_cats: int32 [4, 128, 1], replicated, may hold values from 0 to 63; in each aligned block of 128 rows (0 to 127, 128 to 255, ..., all dimensions but the last counted through in order) at most 2 rows name the same one
- cat_slot: int32 [64], replicated, may hold values from 0 to 63, each once
- neg_index: int32 [4, 128, 128], replicated, may hold values from 0 to 255
Outputs:
- uniting_grad: float32 [3584, 1024], P('dp')
- codebook_grad: float32 [64, 2, 256, 1024], P('dp')
- owner_loss: float32 [64], P('dp')
Inputs may be any that keep to these rules, and one draw needn't show every extreme that they name: `item_cats`: within one row of 128 no category appears more than 2 times, and in some row some category appears exactly 2 times. `cat_slot`: A permutation: every category has its own slot; slot t lies with owner t.
All inputs are finite; a program needn't handle non-finite values.
Results may differ from a plain program's by a relative error of at most 0.028.
Values may be sent and summed in bfloat16 or wider, within the bound.
A program may use at most 128 MiB of HBM per device.

v0:
```python
import math
import jax
import jax.numpy as jnp
from jax import lax
from jax.sharding import PartitionSpec as P

HEAD_IMG = 64
HEAD_TXT = 128
CAP = 2
norm_eps = 1e-06
rope_theta = 1000000.0
contrast_temp = 0.1
beta_weight = 1.0
highest = lax.Precision.HIGHEST


def gelu_value(inputs_f):
    return 0.5 * inputs_f * (1.0 + lax.erf(inputs_f / math.sqrt(2.0)))


def gelu_slope(inputs_f):
    return 0.5 * (1.0 + lax.erf(inputs_f / math.sqrt(2.0))) + inputs_f * jnp.exp(
        -0.5 * inputs_f * inputs_f
    ) / math.sqrt(2.0 * math.pi)


def rotate_pairs(tensor, positions):
    half_dim = tensor.shape[-1] // 2
    exponents = jnp.arange(half_dim).astype(jnp.float32) * (2.0 / tensor.shape[-1])
    inverse_freq = jnp.exp(-math.log(rope_theta) * exponents)
    angles = positions[:, None] * inverse_freq[None, :]
    cosine = jnp.concatenate([jnp.cos(angles), jnp.cos(angles)], axis=-1)[:, None, :]
    sine = jnp.concatenate([jnp.sin(angles), jnp.sin(angles)], axis=-1)[:, None, :]
    rotated = jnp.concatenate([-tensor[..., half_dim:], tensor[..., :half_dim]], axis=-1)
    return tensor * cosine + rotated * sine


def softmax_rows(scores):
    scores = scores - jnp.max(scores, axis=-1, keepdims=True)
    exp_scores = jnp.exp(scores)
    return (exp_scores / jnp.sum(exp_scores, axis=-1, keepdims=True)).astype(jnp.bfloat16)


def image_attention(images, flat_slot):
    item_count, patch_count, model_width = images.shape
    half_width = model_width // 2
    head_count = half_width // HEAD_IMG
    qkv_size = model_width * 3 * half_width
    w_qkv = flat_slot[:qkv_size].reshape(model_width, 3 * half_width)
    w_out = flat_slot[qkv_size : qkv_size + half_width * model_width].reshape(
        half_width, model_width
    )
    float_tokens = images.astype(jnp.float32)
    centred = float_tokens - jnp.mean(float_tokens, axis=-1, keepdims=True)
    variance = jnp.mean(centred * centred, axis=-1, keepdims=True)
    normed = (centred * lax.rsqrt(variance + norm_eps)).astype(jnp.bfloat16)
    projections = jnp.einsum(
        "bpd,de->bpe", normed, w_qkv, preferred_element_type=jnp.float32
    ).astype(jnp.bfloat16)
    queries = projections[..., :half_width].reshape(item_count, patch_count, head_count, HEAD_IMG)
    key_rows = projections[..., half_width : 2 * half_width].reshape(
        item_count, patch_count, head_count, HEAD_IMG
    )
    value_rows = projections[..., 2 * half_width :].reshape(
        item_count, patch_count, head_count, HEAD_IMG
    )
    scores = jnp.einsum(
        "bqhc,bkhc->bhqk", queries, key_rows, preferred_element_type=jnp.float32
    ) / math.sqrt(HEAD_IMG)
    probabilities = softmax_rows(scores)
    attended = jnp.einsum(
        "bhqk,bkhc->bqhc", probabilities, value_rows, preferred_element_type=jnp.float32
    ).astype(jnp.bfloat16)
    attended = attended.reshape(item_count, patch_count, half_width)
    projected = jnp.einsum("bpc,cd->bpd", attended, w_out, preferred_element_type=jnp.float32)
    return jnp.mean(projected, axis=1)


def text_attention(texts, flat_slot):
    item_count, token_count, model_width = texts.shape
    half_width = model_width // 2
    head_count = half_width // HEAD_TXT
    inner_width = half_width + 2 * HEAD_TXT
    qkv_size = model_width * inner_width
    w_qkv = flat_slot[:qkv_size].reshape(model_width, inner_width)
    w_out = flat_slot[qkv_size : qkv_size + half_width * model_width].reshape(
        half_width, model_width
    )
    float_tokens = texts.astype(jnp.float32)
    normed = (
        float_tokens
        * lax.rsqrt(jnp.mean(float_tokens * float_tokens, axis=-1, keepdims=True) + norm_eps)
    ).astype(jnp.bfloat16)
    projections = jnp.einsum("btd,de->bte", normed, w_qkv, preferred_element_type=jnp.float32)
    positions = jnp.arange(token_count).astype(jnp.float32)
    queries = rotate_pairs(
        projections[..., :half_width].reshape(item_count, token_count, head_count, HEAD_TXT),
        positions,
    ).astype(jnp.bfloat16)
    key_rows = rotate_pairs(
        projections[..., half_width : half_width + HEAD_TXT].reshape(
            item_count, token_count, 1, HEAD_TXT
        ),
        positions,
    )[:, :, 0, :].astype(jnp.bfloat16)
    value_rows = projections[..., half_width + HEAD_TXT :].astype(jnp.bfloat16)
    scores = jnp.einsum(
        "bqhc,bkc->bhqk", queries, key_rows, preferred_element_type=jnp.float32
    ) / math.sqrt(HEAD_TXT)
    causal = jnp.arange(token_count)[:, None] >= jnp.arange(token_count)[None, :]
    scores = jnp.where(causal, scores, -1e30)
    probabilities = softmax_rows(scores)
    attended = jnp.einsum(
        "bhqk,bkc->bqhc", probabilities, value_rows, preferred_element_type=jnp.float32
    ).astype(jnp.bfloat16)
    attended = attended.reshape(item_count, token_count, half_width)
    projected = jnp.einsum("btc,cd->btd", attended, w_out, preferred_element_type=jnp.float32)
    return jnp.mean(projected, axis=1)


def merge_forward(embedded, stacked):
    first_rows = embedded.shape[1]
    float_embed = embedded.astype(jnp.float32)
    normed = (
        float_embed
        * lax.rsqrt(jnp.mean(float_embed * float_embed, axis=1, keepdims=True) + norm_eps)
    ).astype(jnp.bfloat16)
    hidden = jnp.dot(normed, stacked[:first_rows], preferred_element_type=jnp.float32)
    activated = gelu_value(hidden).astype(jnp.bfloat16)
    merged = jnp.dot(activated, stacked[first_rows:], preferred_element_type=jnp.float32).astype(
        jnp.bfloat16
    )
    return (normed, hidden, activated, merged)


def merge_backward(hidden, stacked, out_grad, first_rows):
    w_second = stacked[first_rows:]
    act_grad = lax.dot_general(
        out_grad, w_second, (((1,), (1,)), ((), ())), preferred_element_type=jnp.float32
    )
    return (act_grad * gelu_slope(hidden)).astype(jnp.bfloat16)


def item_loss(merged_row, book_rows, negatives):
    emb_width = merged_row.shape[0]
    quant_tau = math.sqrt(emb_width) / 2.0
    residual = merged_row * lax.rsqrt(jnp.mean(merged_row * merged_row) + norm_eps)
    quantized = jnp.zeros_like(merged_row)
    for level_index in range(book_rows.shape[0]):
        code_rows = book_rows[level_index]
        cross_terms = jnp.dot(code_rows, residual, precision=highest)
        logits = (2.0 * cross_terms - jnp.sum(code_rows * code_rows, axis=1)) / quant_tau
        logits = logits - lax.stop_gradient(jnp.max(logits))
        exp_logits = jnp.exp(logits)
        chosen = jnp.dot(exp_logits / jnp.sum(exp_logits), code_rows, precision=highest)
        residual = residual - chosen
        quantized = quantized + chosen
    recon_error = jnp.mean(residual * residual)
    anchor = quantized * lax.rsqrt(jnp.mean(quantized * quantized) + norm_eps)
    candidates = jnp.concatenate([merged_row[None, :], negatives.astype(jnp.float32)], axis=0)
    cand_unit = candidates * lax.rsqrt(
        jnp.mean(candidates * candidates, axis=1, keepdims=True) + norm_eps
    )
    similarity = jnp.dot(cand_unit, anchor, precision=highest) / (emb_width * contrast_temp)
    top_score = lax.stop_gradient(jnp.max(similarity))
    contrast = top_score + jnp.log(jnp.sum(jnp.exp(similarity - top_score))) - similarity[0]
    return contrast + beta_weight * recon_error


def stacked_term(columns, first_grad, second_grad, in_first):
    contract = (((0,), (0,)), ((), ()))
    first_term = lax.dot_general(columns, first_grad, contract, preferred_element_type=jnp.float32)
    second_term = lax.dot_general(
        columns, second_grad, contract, preferred_element_type=jnp.float32
    )
    return jnp.where(in_first[:, None], first_term, second_term)


def per_device(
    images,
    texts,
    section_weights,
    uniting_weights,
    codebooks,
    neg_bank,
    item_cats,
    cat_slot,
    neg_index,
):
    segment_index = lax.axis_index("segment")
    segment_count = lax.axis_size("segment")
    dp_index = lax.axis_index("dp")
    dp_count = lax.axis_size("dp")
    group_index = segment_index % 2
    item_count = images.shape[0]
    flat_slot = section_weights.reshape(-1)
    residual_flag = jnp.where(group_index == 0, 1.0, 0.0).astype(jnp.float32)

    def image_branch(operands):
        image_rows, text_rows, slot_rows = operands
        pooled = image_attention(image_rows, slot_rows) + residual_flag * jnp.mean(
            image_rows.astype(jnp.float32), axis=1
        )
        return jnp.concatenate(
            [pooled, jnp.zeros((item_count, text_rows.shape[2]), jnp.float32)], axis=1
        )

    def text_branch(operands):
        image_rows, text_rows, slot_rows = operands
        pooled = text_attention(text_rows, slot_rows) + residual_flag * jnp.mean(
            text_rows.astype(jnp.float32), axis=1
        )
        return jnp.concatenate(
            [jnp.zeros((item_count, image_rows.shape[2]), jnp.float32), pooled], axis=1
        )

    packed = lax.cond(segment_index < 2, image_branch, text_branch, (images, texts, flat_slot))
    embedded = lax.psum_scatter(packed, "segment", scatter_dimension=0, tiled=True).astype(
        jnp.bfloat16
    )
    stacked = lax.all_gather(uniting_weights, "dp", axis=0, tiled=True)
    first_rows = embedded.shape[1]
    cat_per_dev = codebooks.shape[0]
    slot_count = cat_per_dev * CAP
    row_total = item_cats.shape[1]
    cats_all = item_cats.reshape(-1)
    entry_count = cats_all.shape[0]
    entry_ids = jnp.arange(entry_count)
    category_match = cats_all[:, None] == jnp.arange(cat_slot.shape[0])[None, :]
    entry_slots = jnp.sum(jnp.where(category_match, cat_slot[None, :], 0), axis=1)
    entry_owner = entry_slots // cat_per_dev
    entry_local = entry_slots % cat_per_dev
    entry_row = entry_ids // row_total
    earlier = entry_ids[None, :] < entry_ids[:, None]
    same_cat = (cats_all[:, None] == cats_all[None, :]) & (entry_row[:, None] == entry_row[None, :])
    entry_rank = jnp.sum(jnp.where(earlier & same_cat, 1, 0), axis=1)
    entry_place = entry_local * CAP + entry_rank
    entry_position = entry_row * slot_count + entry_place
    owned = entry_owner == dp_index
    all_slots = segment_count * slot_count
    slot_match_all = owned[None, :] & (entry_position[None, :] == jnp.arange(all_slots)[:, None])
    view_match = lax.dynamic_slice(
        slot_match_all,
        (segment_index * slot_count, segment_index * row_total),
        (slot_count, row_total),
    )
    view_base = segment_index * row_total
    view_slots = view_match.shape[0]
    selection = view_match.astype(jnp.bfloat16)
    valid = jnp.sum(view_match.astype(jnp.float32), axis=1)
    slot_item = jnp.sum(
        jnp.where(view_match, jnp.arange(view_match.shape[1])[None, :] + view_base, 0), axis=1
    )
    slot_negs = jnp.take(neg_index.reshape(entry_count, -1), slot_item, axis=0)
    slot_local = jnp.arange(view_slots) % slot_count // CAP
    bank_rows = neg_bank.reshape(-1, neg_bank.shape[2])
    negatives = jnp.take(bank_rows, slot_local[:, None] * neg_bank.shape[1] + slot_negs, axis=0)
    loss_scale = 1.0 / math.sqrt(dp_count * item_count)

    def owner_objective(merged_float, books):
        per_row = jax.vmap(item_loss)(merged_float, books[slot_local], negatives)
        return jnp.sum(per_row * valid) * loss_scale

    gathered = jnp.dot(
        selection,
        lax.all_gather(embedded, "dp", axis=0, tiled=True),
        preferred_element_type=jnp.float32,
    )
    gathered = gathered.astype(jnp.bfloat16)
    normed_all, hidden_all, activated_all, merged_all = merge_forward(gathered, stacked)
    loss_local, pullback = jax.vjp(owner_objective, merged_all.astype(jnp.float32), codebooks)
    grad_all, book_grad = pullback(jnp.ones((), jnp.float32))
    out_grad = grad_all.astype(jnp.bfloat16)
    hidden_grad = merge_backward(hidden_all, stacked, out_grad, first_rows)
    joined = jnp.concatenate([normed_all, activated_all], axis=1)
    book_total, loss_owner = lax.psum((book_grad, loss_local), "segment")
    shard_rows = uniting_weights.shape[0]
    shard_start = dp_index * shard_rows
    shard_first = shard_start + jnp.arange(shard_rows) < first_rows
    joined_piece = lax.all_gather(joined, "dp", axis=0, tiled=True)
    first_piece = lax.all_gather(hidden_grad, "dp", axis=0, tiled=True)
    second_piece = lax.all_gather(out_grad, "dp", axis=0, tiled=True)
    columns = lax.dynamic_slice_in_dim(joined_piece, shard_start, shard_rows, 1)
    segment_grad = stacked_term(columns, first_piece, second_piece, shard_first)
    uniting_grad = lax.psum(segment_grad, "segment")
    return (uniting_grad, book_total, loss_owner.reshape(1))


def solution(mesh):
    placed = (
        P("dp", None, None),
        P("dp", None, None),
        P("segment", None, None),
        P("dp", None),
        P("dp", None, None, None),
        P("dp", None, None),
        P(),
        P(),
        P(),
    )
    return jax.shard_map(
        per_device,
        mesh=mesh,
        in_specs=placed,
        out_specs=(P("dp", None), P("dp", None, None, None), P("dp")),
        check_vma=False,
    )
```

profile of v0, /device:TPU:1, one launch (start us, length us, event | category | flops | bytes accessed | tf_op | source)
XLA Modules:
  0.0 945.5 jit_solution(2078119373908854478)
XLA Ops:
  7.2 0.7 all-gather.6.cloned.1.call-update
  8.0 1.3 dynamic-slice
  9.9 64.5 %conditional.1 = (f32[8,2560]{1,0:T(8,128)S(1)}) conditional(s32[]{:T(128)} %convert_element_type.98, (bf16[8,64,1536]{2,1,0:T(8,128)(2,1)}, bf16[2752512]{0:T(1024)(128)(2,1)}, f32[]{:T(128)}) %tuple.55, (bf16[8,256,1024]{2,1,0:T(8,128)(2,1)}, bf16[2752512]{0:T(1024)(128)(2,1)}, f32[]{:T(128)}) %tuple.56), branch_computations={%region_2.8_spmd, %region_8.15_spmd} | conditional | flops 9714018304 | bytes 131555384 | solution.py:217
  10.4 3.0 convert_reduce_fusion.2
  13.4 3.5 fusion.43
  16.9 1.8 slice.87
  18.7 6.8 reshape.489
  25.5 9.9 %convolution_convert_fusion.1 = bf16[8,256,1536]{2,1,0:T(8,128)(2,1)S(1)} fusion(bf16[1024,1536,1]{1,0,2:T(8,128)(2,1)} %reshape.489, bf16[8,256,1024]{2,1,0:T(8,128)(2,1)} %get-tuple-element.27, f32[8,256]{1,0:T(8,128)S(1)} %add_rsqrt_fusion.1, f32[8,256]{1,0:T(8,128)S(1)} %broadcast_multiply_fusion), kind=kOutput, calls=%fused_computation.65 | convolution fusion | flops 6453985280 | bytes 13647872 | tf_op jit(solution)/shard_map/cond/branch_1_fun/bpd,de->bpe/dot_general | solution.py:57
  35.4 2.8 fusion.168
  38.2 4.0 copy.70
  42.2 3.9 copy.71
  46.1 10.6 %fusion.169 = (f32[8,8,256]{2,1,0:T(8,128)S(1)}, f32[8,8,256,256]{2,3,1,0:T(8,128)}) fusion(bf16[8,256,8,64]{1,3,2,0:T(8,128)(2,1)} %bitcast.232, bf16[8,256,8,64]{1,3,2,0:T(8,128)(2,1)} %bitcast.233), kind=kOutput, calls=%fused_computation.284 | convolution fusion | flops 549454080 | bytes 21037056 | tf_op jit(solution)/shard_map/cond/branch_1_fun/sub | solution.py:39
  56.7 2.4 copy.69
  59.1 9.4 fusion.52
  68.4 1.3 slice.92
  70.2 4.0 convolution_reduce_fusion.1
  74.5 13.8 %all-reduce.5 = bf16[8,2560]{1,0:T(8,128)(2,1)S(1)} all-reduce(f32[8,2560]{1,0:T(8,128)S(1)} %get-tuple-element.92), channel_id=2, replica_groups=mesh['segment'=4,'dp'=64] {'segment'}, use_global_device_ids=true, to_apply=%region_15.16.clone | all-reduce | flops 20480 | bytes 122880
  88.3 160.0 %all-gather = bf16[64,2,2560]{2,1,0:T(2,128)(2,1)S(1)} all-gather(bf16[1,2,2560]{2,1,0:T(2,128)(2,1)S(1)} %fusion.106), channel_id=1, replica_groups=mesh['segment'=4,'dp'=64] {'dp'}, dimensions={0}, use_global_device_ids=true | all-gather | bytes 665600 | tf_op jit(solution)/shard_map/all_gather | solution.py:266
  249.5 1.5 gather_fusion
  251.4 2.0 gather_fusion.1
  255.0 1.6 fusion.101
  256.9 3.3 multiply_convert_fusion.1
  260.2 2.1 multiply_reduce_fusion.9
  262.3 1.7 fusion.99
  264.5 1.1 fusion.97
  265.6 1.7 fusion.91
  267.7 0.7 broadcast_divide_fusion
  268.4 0.6 broadcast_divide_fusion.1
  269.1 0.7 broadcast_multiply_fusion.4
  269.7 1.1 fusion.89
  270.9 0.6 multiply_reduce_fusion.2
  271.8 1.8 broadcast_multiply_fusion.2
  273.6 0.9 copy-done.5
  274.5 1.3 fusion.82
  276.0 0.6 bitcast_multiply_fusion
  277.3 0.6 maximum_bitcast_fusion
  278.0 2.2 fusion.80
  280.5 1.9 fusion.87
  282.6 0.7 multiply_negate_fusion.1
  283.3 0.6 broadcast_multiply_fusion.6
  283.9 1.1 fusion.85
  284.9 0.6 negate_add_fusion
  285.6 1.7 fusion.95
  287.5 0.7 multiply_negate_fusion
  288.7 1.8 multiply_reduce_fusion.1
  290.7 1.1 fusion.93
  291.9 0.8 fusion.116
  292.7 0.6 copy-done.16
  293.3 2.2 fusion.77
  295.5 148.0 %all-gather.2 = bf16[64,2,1024]{2,1,0:T(2,128)(2,1)S(1)} all-gather(bf16[1,2,1024]{2,1,0:T(2,128)(2,1)S(1)} %fusion.77), channel_id=1, replica_groups=mesh['segment'=4,'dp'=64] {'dp'}, dimensions={0}, use_global_device_ids=true | all-gather | bytes 266240 | tf_op jit(solution)/shard_map/all_gather | solution.py:281
  443.6 0.8 reshape.482
  444.4 155.0 %all-gather.1 = bf16[64,2,3584]{2,1,0:T(2,128)(2,1)S(1)} all-gather(bf16[1,2,3584]{2,1,0:T(2,128)(2,1)} %maximum_bitcast_fusion), channel_id=1, replica_groups=mesh['segment'=4,'dp'=64] {'dp'}, dimensions={0}, use_global_device_ids=true | all-gather | bytes 931840 | tf_op jit(solution)/shard_map/all_gather | solution.py:280
  599.4 1.3 reshape.480
  600.7 148.5 %all-gather.3 = bf16[64,2,1024]{2,1,0:T(2,128)(2,1)S(1)} all-gather(bf16[1,2,1024]{2,1,0:T(2,128)(2,1)} %bitcast.244), channel_id=1, replica_groups=mesh['segment'=4,'dp'=64] {'dp'}, dimensions={0}, use_global_device_ids=true | all-gather | bytes 266240 | tf_op jit(solution)/shard_map/all_gather | solution.py:282
  749.4 1.2 fusion.58
  751.2 2.2 pad_add_fusion
  754.0 4.5 scatter_fusion
  758.5 1.2 fusion.104
  759.8 1.8 convolution_select_fusion
  761.7 1.3 fusion.149
  763.6 116.9 %psum.23 = f32[1]{0:T(128)} all-reduce(f32[1]{0:T(128)} %bitcast.57), channel_id=1, replica_groups=mesh['segment'=4,'dp'=64] {'segment'}, use_global_device_ids=true, to_apply=%region_40.41 | all-reduce | flops 1 | bytes 8 | tf_op jit(solution)/shard_map/psum | solution.py:276
  880.5 53.2 %all-reduce.9.cloned.1.call-done = (f32[56,1024]{1,0:T(8,128)}, f32[1,2,256,1024]{3,2,1,0:T(8,128)}) async-done(((f32[56,1024]{1,0:T(8,128)}, f32[1,2,256,1024]{3,2,1,0:T(8,128)}), (f32[56,1024]{1,0:T(8,128)}, f32[1,2,256,1024]{3,2,1,0:T(8,128)})) %all-reduce.9.cloned.1.call-update) | async-done | bytes 2326544 | tf_op jit(solution)/shard_map/psum | solution.py:285
  933.7 1.6 copy.189
  935.3 3.2 copy.190
  (135 shorter events, 9.2 us)
Async XLA Ops:
  7.2 244.2 %copy-start = (bf16[1,256,1024]{2,1,0:T(8,128)(2,1)S(1)}, bf16[1,256,1024]{2,1,0:T(8,128)(2,1)}, u32[]{:S(2)}) copy-start(bf16[1,256,1024]{2,1,0:T(8,128)(2,1)} %param.16) | copy-start | bytes 1572868
  7.2 249.7 %all-gather.6.cloned.1.call-start = ((), (), s32[]{:S(2)}) async-start(), calls=%async_computation | async-start | bytes 7454720 | tf_op jit(solution)/shard_map/all_gather | solution.py:221
  7.9 925.8 %all-reduce.9.cloned.1.call-start = ((), (), s32[]{:S(2)}) async-start(), calls=%async_computation.1 | async-start | bytes 4653056 | tf_op jit(solution)/shard_map/psum | solution.py:285
  10.4 6.5 copy-start.4
  74.4 174.1 %copy-start.15 = (s32[4,128,1]{1,2,0:T(1,128)S(1)}, s32[4,128,1]{1,2,0:T(1,128)}, u32[]{:S(2)}) copy-start(s32[4,128,1]{1,2,0:T(1,128)} %param.17) | copy-start | bytes 6148
  74.5 174.1 %copy-start.28 = (s32[64]{0:T(128)S(1)}, s32[64]{0:T(128)}, u32[]{:S(2)}) copy-start(s32[64]{0:T(128)} %param.18) | copy-start | bytes 772
  249.4 27.3 %copy-start.24 = (f32[2]{0:T(128)}, f32[2]{0:T(128)S(1)}, u32[]{:S(2)}) copy-start(f32[2]{0:T(128)S(1)} %get-tuple-element.44) | copy-start | bytes 28
  251.3 3.1 copy-start.6
  253.3 1.7 copy-start.8
  254.4 2.2 copy-start.7
  262.3 8.6 copy-start.2
  271.8 8.5 copy-start.11
  273.6 1.0 copy-start.5
  276.6 10.7 %copy-start.17 = (f32[2]{0:T(128)}, f32[2]{0:T(128)S(1)}, u32[]{:S(2)}) copy-start(f32[2]{0:T(128)S(1)} %get-tuple-element.72) | copy-start | bytes 28
  276.6 0.6 copy-start.22
  278.0 10.7 %copy-start.3 = (f32[2,128,1024]{2,0,1:T(2,128)S(1)}, f32[2,128,1024]{2,0,1:T(2,128)}, u32[]{:S(2)}) copy-start(f32[2,128,1024]{2,0,1:T(2,128)} %fusion.101) | copy-start | bytes 3145732
  285.6 6.2 copy-start.12
  285.6 6.3 slice-start
  292.7 0.6 copy-start.16
  600.7 149.9 %copy-start.13 = (f32[2,1024]{1,0:T(2,128)S(1)}, f32[2,1024]{1,0:T(2,128)}, u32[]{:S(2)}) copy-start(f32[2,1024]{1,0:T(2,128)} %copy-done.12) | copy-start | bytes 24580
  600.7 149.9 %copy-start.14 = (f32[2,1024]{1,0:T(2,128)S(1)}, f32[2,1024]{1,0:T(2,128)}, u32[]{:S(2)}) copy-start(f32[2,1024]{1,0:T(2,128)} %broadcast_multiply_fusion.4) | copy-start | bytes 24580
  600.7 149.9 %copy-start.19 = (f32[2,256]{1,0:T(2,128)S(1)}, f32[2,256]{1,0:T(2,128)}, u32[]{:S(2)}) copy-start(f32[2,256]{1,0:T(2,128)} %get-tuple-element.76) | copy-start | bytes 6148
  600.7 149.9 %copy-start.20 = (f32[2,256]{1,0:T(2,128)S(1)}, f32[2,256]{1,0:T(2,128)}, u32[]{:S(2)}) copy-start(f32[2,256]{1,0:T(2,128)} %broadcast_divide_fusion.1) | copy-start | bytes 6148
  600.7 149.9 %copy-start.21 = (f32[2,256]{1,0:T(2,128)S(1)}, f32[2,256]{1,0:T(2,128)}, u32[]{:S(2)}) copy-start(f32[2,256]{1,0:T(2,128)} %get-tuple-element.38) | copy-start | bytes 6148
  753.4 0.6 copy-start.27
  754.0 4.5 copy-start.10
  754.0 5.8 copy-start.29
  758.5 3.1 copy-start.1
  758.5 3.2 copy-start.18
  758.5 3.2 copy-start.23
  758.5 3.2 copy-start.25
  758.5 3.2 copy-start.26
Sparse Core Ops, SparseCore 0:
  11.5 144.8 all-gather.5
  761.8 171.8 all-reduce.8
where the time goes:
time: 953 us; the launch traced here: 946 us
  blocking collectives  742 us (78%)
  matrix products  59.7 us (6%)
  waiting for transfers between devices  53.9 us (6%)
  local copies, waits for them, and re-layouts  39.2 us (4%)
  other arithmetic  33.6 us (4%)
  between operations  16.1 us (2%)
    all_gather x1, blocking collectives, per_device(): lax.all_gather(embedded, 'dp', axis=0, tiled=True)  160 us
    all_gather x1, blocking collectives, per_device(): joined_piece = lax.all_gather(joined, 'dp', axis=0, tiled=True)  155 us
    all_gather x1, blocking collectives, per_device(): second_piece = lax.all_gather(out_grad, 'dp', axis=0, tiled=True)  149 us
    all_gather x1, blocking collectives, per_device(): first_piece = lax.all_gather(hidden_grad, 'dp', axis=0, tiled=True)  148 us
    psum x1, blocking collectives, per_device(): book_total, loss_owner = lax.psum((book_grad, loss_local), 'segment')  117 us
    psum x1, waiting for transfers between devices, per_device(): uniting_grad = lax.psum(segment_grad, 'segment')  53.2 us
  transfers between devices with their start and end apart: 2, of which 1 were waited for; matrix products, arithmetic and copies ran while one was open for 8% of the time, Pallas kernels for 0%

commit v1 on v0

--- a/solution.py
+++ b/solution.py
@@ -282,7 +282,7 @@
     second_piece = lax.all_gather(out_grad, "dp", axis=0, tiled=True)
     columns = lax.dynamic_slice_in_dim(joined_piece, shard_start, shard_rows, 1)
     segment_grad = stacked_term(columns, first_piece, second_piece, shard_first)
-    uniting_grad = lax.psum(segment_grad, "segment")
+    uniting_grad = jnp.sum(lax.all_gather(segment_grad, "segment"), axis=0)
     return (uniting_grad, book_total, loss_owner.reshape(1))
 
 

time: 953 us -> 900 us (0.944)
  waiting for transfers between devices: 53.9 us -> 0.72 us
    all_gather x0 -> x1, blocking collectives: none -> 91.8 us  [per_device(): uniting_grad = jnp.sum(lax.all_gather(segment_grad, 'segment'), axis=0)]
    psum x1, blocking collectives: 117 us -> 34.7 us  [per_device(): book_total, loss_owner = lax.psum((book_grad, loss_local), 'segment')]
    psum x1, waiting for transfers between devices: 53.2 us -> 0.01 us  [per_device(): book_total, loss_owner = lax.psum((book_grad, loss_local), 'segment')]
  transfers between devices with their start and end apart: 2 -> 2, of which waited for: 1 -> 0; matrix products, arithmetic and copies ran while one was open for 8% -> 9% of each run, Pallas kernels for 0% -> 0%
where the time goes in v1:
time: 900 us; the launch traced here: 893 us
  blocking collectives  751 us (83%)
  matrix products  57.1 us (6%)
  local copies, waits for them, and re-layouts  37.4 us (4%)
  other arithmetic  29.7 us (3%)
  between operations  16 us (2%)
    all_gather x1, blocking collectives, per_device(): lax.all_gather(embedded, 'dp', axis=0, tiled=True)  160 us
    all_gather x1, blocking collectives, per_device(): joined_piece = lax.all_gather(joined, 'dp', axis=0, tiled=True)  155 us
    all_gather x1, blocking collectives, per_device(): first_piece = lax.all_gather(hidden_grad, 'dp', axis=0, tiled=True)  148 us
    all_gather x1, blocking collectives, per_device(): second_piece = lax.all_gather(out_grad, 'dp', axis=0, tiled=True)  148 us
    all_gather x1, blocking collectives, per_device(): uniting_grad = jnp.sum(lax.all_gather(segment_grad, 'segment'), axis=0)  91.8 us
    psum x1, blocking collectives, per_device(): book_total, loss_owner = lax.psum((book_grad, loss_local), 'segment')  34.7 us
  transfers between devices with their start and end apart: 2, of which 0 were waited for; matrix products, arithmetic and copies ran while one was open for 9% of the time, Pallas kernels for 0%

profile of v1, /device:TPU:1, one launch (start us, length us, event | category | flops | bytes accessed | tf_op | source)
XLA Modules:
  0.0 893.1 jit_solution(15912746876364897428)
XLA Ops:
  7.2 0.7 all-gather.7.cloned.1.call-update
  8.0 1.3 dynamic-slice
  9.9 64.5 %conditional.1 = (f32[8,2560]{1,0:T(8,128)S(1)}) conditional(s32[]{:T(128)} %convert_element_type.98, (bf16[8,64,1536]{2,1,0:T(8,128)(2,1)}, bf16[2752512]{0:T(1024)(128)(2,1)}, f32[]{:T(128)}) %tuple.54, (bf16[8,256,1024]{2,1,0:T(8,128)(2,1)}, bf16[2752512]{0:T(1024)(128)(2,1)}, f32[]{:T(128)}) %tuple.55), branch_computations={%region_2.8_spmd, %region_8.15_spmd} | conditional | flops 9714018304 | bytes 131555384 | solution.py:217
  10.4 3.0 convert_reduce_fusion.2
  13.4 3.5 fusion.43
  16.9 1.8 slice.87
  18.7 6.8 reshape.490
  25.5 9.9 %convolution_convert_fusion.1 = bf16[8,256,1536]{2,1,0:T(8,128)(2,1)S(1)} fusion(bf16[1024,1536,1]{1,0,2:T(8,128)(2,1)} %reshape.490, bf16[8,256,1024]{2,1,0:T(8,128)(2,1)} %get-tuple-element.27, f32[8,256]{1,0:T(8,128)S(1)} %add_rsqrt_fusion.1, f32[8,256]{1,0:T(8,128)S(1)} %broadcast_multiply_fusion), kind=kOutput, calls=%fused_computation.65 | convolution fusion | flops 6453985280 | bytes 13647872 | tf_op jit(solution)/shard_map/cond/branch_1_fun/bpd,de->bpe/dot_general | solution.py:57
  35.4 2.8 fusion.168
  38.2 4.0 copy.70
  42.2 3.9 copy.71
  46.1 10.6 %fusion.169 = (f32[8,8,256]{2,1,0:T(8,128)S(1)}, f32[8,8,256,256]{2,3,1,0:T(8,128)}) fusion(bf16[8,256,8,64]{1,3,2,0:T(8,128)(2,1)} %bitcast.234, bf16[8,256,8,64]{1,3,2,0:T(8,128)(2,1)} %bitcast.235), kind=kOutput, calls=%fused_computation.284 | convolution fusion | flops 549454080 | bytes 21037056 | tf_op jit(solution)/shard_map/cond/branch_1_fun/sub | solution.py:39
  56.7 2.4 copy.69
  59.0 9.4 %fusion.52 = bf16[8,8,64,256]{3,2,1,0:T(8,128)(2,1)} fusion(bf16[8,256,8,64]{1,3,2,0:T(8,128)(2,1)} %bitcast.236, f32[8,8,256,256]{2,3,1,0:T(8,128)} %get-tuple-element.64, f32[8,8,256]{2,1,0:T(8,128)S(1)} %get-tuple-element.63), kind=kOutput, calls=%fused_computation.70 | convolution fusion | flops 546308096 | bytes 21037056 | tf_op jit(solution)/shard_map/cond/branch_1_fun/bhqk,bkhc->bqhc/dot_general | solution.py:71
  68.4 1.3 slice.92
  69.7 0.5 reshape.491
  70.2 4.0 convolution_reduce_fusion.1
  74.4 13.8 %all-reduce.5 = bf16[8,2560]{1,0:T(8,128)(2,1)S(1)} all-reduce(f32[8,2560]{1,0:T(8,128)S(1)} %get-tuple-element.88), channel_id=3, replica_groups=mesh['segment'=4,'dp'=64] {'segment'}, use_global_device_ids=true, to_apply=%region_15.16.clone | all-reduce | flops 20480 | bytes 122880
  88.3 160.0 %all-gather.1 = bf16[64,2,2560]{2,1,0:T(2,128)(2,1)S(1)} all-gather(bf16[1,2,2560]{2,1,0:T(2,128)(2,1)S(1)} %fusion.106), channel_id=1, replica_groups=mesh['segment'=4,'dp'=64] {'dp'}, dimensions={0}, use_global_device_ids=true | all-gather | bytes 665600 | tf_op jit(solution)/shard_map/all_gather | solution.py:266
  248.3 0.2 reshape.479
  248.8 0.3 select_reduce_fusion
  249.5 1.5 gather_fusion
  251.4 2.0 gather_fusion.1
  253.4 0.2 multiply_reduce_fusion.4
  253.6 0.3 multiply_reduce_fusion.5
  253.9 0.5 copy-done.7
  254.4 1.6 fusion.101
  256.0 0.2 slice_bitcast_fusion.3
  256.3 3.3 multiply_convert_fusion.1
  259.6 2.1 multiply_reduce_fusion.9
  261.8 1.7 fusion.99
  263.9 1.1 fusion.97
  265.1 1.7 fusion.91
  267.4 1.1 fusion.89
  268.6 0.6 multiply_reduce_fusion.2
  269.5 1.8 broadcast_multiply_fusion.2
  271.3 0.9 copy-done.4
  272.2 1.3 fusion.82
  274.0 2.1 fusion.80
  276.3 1.9 fusion.87
  278.2 0.2 fusion.130
  278.6 1.1 fusion.85
  279.8 0.6 fusion.149
  281.0 34.7 %psum.15 = f32[1]{0:T(128)} all-reduce(f32[1]{0:T(128)} %bitcast.58), channel_id=1, replica_groups=mesh['segment'=4,'dp'=64] {'segment'}, use_global_device_ids=true, to_apply=%region_40.41 | all-reduce | flops 1 | bytes 8 | tf_op jit(solution)/shard_map/psum | solution.py:276
  315.7 1.7 fusion.95
  317.7 0.5 fusion.58
  318.3 0.5 fusion.60
  318.8 2.2 pad_add_fusion
  321.0 1.6 broadcast.671
  322.6 8.0 scatter_fusion
  330.7 1.2 copy-done.2
  331.9 1.8 multiply_reduce_fusion.1
  333.9 1.1 fusion.93
  335.1 0.8 fusion.116
  335.9 2.2 fusion.77
  338.1 148.5 %all-gather.3 = bf16[64,2,1024]{2,1,0:T(2,128)(2,1)S(1)} all-gather(bf16[1,2,1024]{2,1,0:T(2,128)(2,1)S(1)} %fusion.77), channel_id=1, replica_groups=mesh['segment'=4,'dp'=64] {'dp'}, dimensions={0}, use_global_device_ids=true | all-gather | bytes 266240 | tf_op jit(solution)/shard_map/all_gather | solution.py:281
  486.7 154.5 %all-gather.2 = bf16[64,2,3584]{2,1,0:T(2,128)(2,1)S(1)} all-gather(bf16[1,2,3584]{2,1,0:T(2,128)(2,1)S(1)} %maximum_bitcast_fusion), channel_id=1, replica_groups=mesh['segment'=4,'dp'=64] {'dp'}, dimensions={0}, use_global_device_ids=true | all-gather | bytes 931840 | tf_op jit(solution)/shard_map/all_gather | solution.py:280
  641.2 0.3 reshape.481
  641.6 148.0 %all-gather.4 = bf16[64,2,1024]{2,1,0:T(2,128)(2,1)S(1)} all-gather(bf16[1,2,1024]{2,1,0:T(2,128)(2,1)S(1)} %bitcast.246), channel_id=1, replica_groups=mesh['segment'=4,'dp'=64] {'dp'}, dimensions={0}, use_global_device_ids=true | all-gather | bytes 266240 | tf_op jit(solution)/shard_map/all_gather | solution.py:282
  789.7 0.3 fusion.104
  790.0 0.3 convolution_select_fusion
  790.3 91.8 %all-gather = f32[224,1024]{1,0:T(8,128)S(1)} all-gather(f32[56,1024]{1,0:T(8,128)S(1)} %convolution_select_fusion), channel_id=2, replica_groups=mesh['segment'=4,'dp'=64] {'segment'}, dimensions={0}, use_global_device_ids=true | all-gather | bytes 1146880 | tf_op jit(solution)/shard_map/all_gather | solution.py:285
  882.1 0.7 reduce_sum.318
  882.8 3.2 copy.188
  (100 shorter events, 4.4 us)
Async XLA Ops:
  7.2 244.2 %copy-start = (bf16[1,256,1024]{2,1,0:T(8,128)(2,1)S(1)}, bf16[1,256,1024]{2,1,0:T(8,128)(2,1)}, u32[]{:S(2)}) copy-start(bf16[1,256,1024]{2,1,0:T(8,128)(2,1)} %param.16) | copy-start | bytes 1572868
  7.2 249.1 %all-gather.7.cloned.1.call-start = ((), (), s32[]{:S(2)}) async-start(), calls=%async_computation | async-start | bytes 7454720 | tf_op jit(solution)/shard_map/all_gather | solution.py:221
  7.9 874.9 %all-reduce.8.cloned.1.call-start = ((), (), s32[]{:S(2)}) async-start(), calls=%async_computation.1 | async-start | bytes 4194304 | tf_op jit(solution)/shard_map/psum | solution.py:276
  10.4 6.5 copy-start.3
  74.4 174.2 %copy-start.11 = (s32[4,128,1]{1,2,0:T(1,128)S(1)}, s32[4,128,1]{1,2,0:T(1,128)}, u32[]{:S(2)}) copy-start(s32[4,128,1]{1,2,0:T(1,128)} %param.17) | copy-start | bytes 6148
  74.4 174.2 %copy-start.12 = (s32[64]{0:T(128)S(1)}, s32[64]{0:T(128)}, u32[]{:S(2)}) copy-start(s32[64]{0:T(128)} %param.18) | copy-start | bytes 772
  251.3 2.0 copy-start.5
  253.3 1.0 copy-start.7
  253.4 2.6 copy-start.6
  261.8 6.8 copy-start.1
  269.5 6.6 copy-start.10
  271.3 1.0 copy-start.4
  330.7 1.2 copy-start.2
  331.9 3.2 slice-start
Sparse Core Ops, SparseCore 0:
  11.5 144.8 all-gather.6
  330.8 57.1 all-reduce.7
